TPU v7x, 128 devices: a whole 4x4x4 slice. The times are simulated.
128 devices in a mesh: dp: 8 (over z, x_hi), ctx: 16 (over x_lo, y, core).
Axes of the slice: x: 4 (x_hi: 2, x_lo: 2; x = x_hi * 2 + x_lo), y: 4, z: 4, core: 2. Of those that a mesh axis runs over, the one named last changes fastest.
Arguments:
- events: bfloat16 [65536, 1024], P(('dp', 'ctx')), parts along dimension 0, may hold values from -48 to 48
- destination: int32 [65536], P(('dp', 'ctx')), parts along dimension 0, may hold values from 0 to 8191, as said below
- segment: int32 [65536], P(('dp', 'ctx')), parts along dimension 0, may hold values from 0 to 3, never falling along the last dimension, each value on 1 to 6144 neighbouring positions
- w_query: bfloat16 [1024, 1024], replicated, may hold values from -0.375 to 0.375
- key_weight: bfloat16 [1024, 256], replicated, may hold values from -0.1875 to 0.1875
- value_weight: bfloat16 [1024, 256], replicated, may hold values from -0.75 to 0.75
Outputs:
- attended: bfloat16 [65536, 1024], P(('dp', 'ctx')), parts along dimension 0
There are 8 independent parts, one for each index of `dp`. A program takes and returns all parts, laid end to end along the dimension named above; an argument that names none is the same for every part. Nothing has to cross between parts.
Inputs may be any that keep to these rules, and one draw needn't show every extreme that they name: destination is a permutation that moves stored events in aligned blocks of 64 rows, keeping their order inside a block; the 8 blocks of one device land on 8 different devices' ranges of 512 packed positions, so at most 64 rows of one device reach one device's range.
All inputs are finite; a program needn't handle non-finite values.
Results may differ from a plain program's by a relative error of at most 0.0045.
The roundings to bfloat16 on the way count: a program that leaves them out, or rounds other values in their place, can miss the bound.
Values may be sent and summed in bfloat16 or wider, within the bound.
No kernel may reach another device: no remote copies, remote signals or barrier semaphores. Data moves between devices by JAX's collectives and lax.ppermute only.
A program may use at most 64 MiB of HBM per device.

v0:
```python
import math
import jax
import jax.numpy as jnp
from jax import lax
from jax.sharding import PartitionSpec as P

QUERY_HEADS = 8
KEY_VALUE_HEADS = 2
HEAD_SIZE = 128
BLOCKS = 8
NEGATIVE_FILL = -1e30


def on_device(events, destination, segment, w_query, key_weight, value_weight):
    token_count = events.shape[0]
    width = events.shape[1]
    ndevices = lax.axis_size("ctx")
    myself = lax.axis_index("ctx")
    group_size = QUERY_HEADS // KEY_VALUE_HEADS
    score_scale = 1.0 / math.sqrt(HEAD_SIZE)
    lanes = jnp.arange(ndevices, dtype=jnp.int32)
    local_rows = jnp.arange(token_count, dtype=jnp.int32)
    target = destination // token_count
    place = destination % token_count
    bucket = token_count // BLOCKS
    own_position = myself * token_count + local_rows
    onehot = (target[:, None] == lanes[None, :]).astype(jnp.int32)
    before = jnp.cumsum(onehot, axis=0) - onehot
    slot = jnp.sum(before * onehot, axis=1)
    index = target * bucket + slot
    send_rows = (
        jnp.zeros((ndevices * bucket, width), events.dtype)
        .at[index]
        .set(events)
        .reshape(ndevices, bucket, width)
    )
    send_place = (
        jnp.full((ndevices * bucket,), token_count, jnp.int32)
        .at[index]
        .set(place)
        .reshape(ndevices, bucket)
    )
    got_rows, got_place = (
        lax.all_to_all(send_rows, "ctx", split_axis=0, concat_axis=0, tiled=True),
        lax.all_to_all(send_place, "ctx", split_axis=0, concat_axis=0, tiled=True),
    )
    packed = (
        jnp.zeros((token_count, width), events.dtype)
        .at[got_place.reshape(-1)]
        .set(got_rows.reshape(-1, width), mode="drop")
    )
    query_rows = jnp.dot(packed, w_query, preferred_element_type=jnp.float32).astype(jnp.bfloat16)
    key_rows = jnp.dot(packed, key_weight, preferred_element_type=jnp.float32).astype(jnp.bfloat16)
    value_rows = jnp.dot(packed, value_weight, preferred_element_type=jnp.float32).astype(
        jnp.bfloat16
    )
    query_head_rows = query_rows.reshape(token_count, KEY_VALUE_HEADS, group_size, HEAD_SIZE)
    query_seg = segment.astype(jnp.float32)
    seg_sent = segment.astype(jnp.bfloat16)
    start_state = (
        jnp.full((KEY_VALUE_HEADS, group_size, token_count), NEGATIVE_FILL, jnp.float32),
        jnp.zeros((KEY_VALUE_HEADS, group_size, token_count), jnp.float32),
        jnp.zeros((KEY_VALUE_HEADS, group_size, token_count, HEAD_SIZE), jnp.float32),
    )
    carry = start_state
    key_portion = lax.all_gather(key_rows, "ctx", axis=0, tiled=True)
    value_portion = lax.all_gather(value_rows, "ctx", axis=0, tiled=True)
    seg_piece = lax.all_gather(seg_sent, "ctx", axis=0, tiled=True)
    token_rows = key_portion.shape[0]
    block_step = 512
    event_count = token_rows // block_step
    key_block_list = key_portion.reshape(event_count, block_step, KEY_VALUE_HEADS, HEAD_SIZE)
    value_block_list = value_portion.reshape(event_count, block_step, KEY_VALUE_HEADS, HEAD_SIZE)
    seg_blocks = seg_piece.astype(jnp.float32).reshape(event_count, block_step)
    offsets = jnp.arange(event_count, dtype=jnp.int32) * block_step

    def one_block(state, inputs):
        key_tile_rows, value_block, seg_block, offset = inputs
        key_pos = offset + jnp.arange(block_step, dtype=jnp.int32)
        allowed = (seg_block[None, :] == query_seg[:, None]) & (
            key_pos[None, :] <= own_position[:, None]
        )
        best, total_tokens, accum = state
        logit_scores = (
            jnp.einsum(
                "qxli,oxi->xlqo", query_head_rows, key_tile_rows, preferred_element_type=jnp.float32
            )
            * score_scale
        )
        logit_scores = jnp.where(allowed, logit_scores, NEGATIVE_FILL)
        fresh = jnp.maximum(best, jnp.max(logit_scores, axis=-1))
        softmax_weights = jnp.where(allowed, jnp.exp(logit_scores - fresh[..., None]), 0.0)
        shrink = jnp.exp(best - fresh)
        total_tokens = total_tokens * shrink + jnp.sum(softmax_weights, axis=-1)
        accum = accum * shrink[..., None] + jnp.einsum(
            "qlwc,cqh->qlwh",
            softmax_weights.astype(jnp.bfloat16),
            value_block,
            preferred_element_type=jnp.float32,
        )
        state = (fresh, total_tokens, accum)
        return (state, None)

    carry, _ = lax.scan(one_block, carry, (key_block_list, value_block_list, seg_blocks, offsets))
    best, total_tokens, accum = carry
    result = (
        (accum / total_tokens[..., None])
        .transpose(2, 0, 1, 3)
        .reshape(token_count, QUERY_HEADS * HEAD_SIZE)
        .astype(jnp.bfloat16)
    )
    return result


def solution(mesh):
    return jax.shard_map(
        on_device,
        mesh=mesh,
        in_specs=(P(("dp", "ctx"), None), P(("dp", "ctx")), P(("dp", "ctx")), P(), P(), P()),
        out_specs=P(("dp", "ctx"), None),
        check_vma=False,
    )
```

profile of v0, /device:TPU:1, one launch (start us, length us, event | category | flops | bytes accessed | tf_op | source)
XLA Modules:
  0.0 347.3 jit_solution(6097771895671642066)
XLA Ops:
  8.9 2.4 scatter_custom_fusion
  12.0 6.9 %all-to-all-start = ((s32[16,1,64]{2,1,0:T(1,128)}), s32[16,1,64]{2,1,0:T(1,128)S(1)}, u32[]{:S(2)}, u32[]{:S(2)}) async-start(s32[16,1,64]{2,1,0:T(1,128)} %all_to_all.9), calls=%async_computation | async-start | bytes 16384 | tf_op jit(solution)/shard_map/all_to_all | solution.py:45
  18.9 4.8 %scatter_custom_fusion.1 = bf16[1024,1024]{1,0:T(8,128)(2,1)} fusion(s32[512]{0:T(512)S(1)} %compare_select_fusion.1, bf16[512,1024]{1,0:T(8,128)(2,1)} %param.8, bf16[]{:T(256)} %constant.62.clone.1), kind=kCustom, calls=%fused_computation.33 | custom fusion | bytes 2097664 | tf_op jit(solution)/shard_map/scatter | solution.py:34
  24.4 5.2 %all-to-all-start.1 = ((bf16[16,64,1024]{2,1,0:T(8,128)(2,1)}), bf16[16,64,1024]{2,1,0:T(8,128)(2,1)}, u32[]{:S(2)}, u32[]{:S(2)}) async-start(bf16[16,64,1024]{2,1,0:T(8,128)(2,1)} %bitcast.83), calls=%async_computation.1 | async-start | bytes 4194304 | tf_op jit(solution)/shard_map/all_to_all | solution.py:44
  30.9 26.4 %all-to-all-done.1 = bf16[16,64,1024]{2,1,0:T(8,128)(2,1)} async-done(((bf16[16,64,1024]{2,1,0:T(8,128)(2,1)}), bf16[16,64,1024]{2,1,0:T(8,128)(2,1)}, u32[]{:S(2)}, u32[]{:S(2)}) %all-to-all-start.1) | async-done | bytes 2097184 | tf_op jit(solution)/shard_map/all_to_all | solution.py:44
  57.3 6.2 %scatter_custom_fusion.2 = bf16[512,1024]{1,0:T(8,128)(2,1)S(1)} fusion(s32[1024]{0:T(1024)S(1)} %bitcast.87, bf16[1024,1024]{1,0:T(8,128)(2,1)} %bitcast.4, bf16[]{:T(256)} %constant.62.clone.1), kind=kCustom, calls=%fused_computation.36 | custom fusion | bytes 1049088 | tf_op jit(solution)/shard_map/scatter | solution.py:50
  63.4 2.2 convolution_convert_fusion.1
  65.7 2.2 convolution_convert_fusion.2
  68.0 21.0 %all-gather = bf16[16,1,512]{2,1,0:T(2,128)(2,1)S(1)} all-gather(bf16[1,1,512]{2,1,0:T(2,128)(2,1)S(1)} %reshape.121), channel_id=1, replica_groups=mesh['dp'=8,'ctx'=16] {'ctx'}, dimensions={0}, use_global_device_ids=true | all-gather | bytes 17408 | tf_op jit(solution)/shard_map/all_gather | solution.py:68
  89.0 2.2 convolution_convert_fusion
  91.2 2.6 reshape.91
  95.2 11.1 %all-gather.6.cloned.1.call-done = bf16[8192,256]{1,0:T(8,128)(2,1)} async-done(((bf16[512,256]{1,0:T(8,128)(2,1)}), bf16[8192,256]{1,0:T(8,128)(2,1)}) %all-gather.6.cloned.1.call-update) | async-done | bytes 4194320 | tf_op jit(solution)/shard_map/all_gather | solution.py:67
  106.3 6.9 %reshape.92 = bf16[16,512,2,128]{3,2,1,0:T(2,128)(2,1)} reshape(bf16[8192,256]{1,0:T(8,128)(2,1)} %all-gather.6.cloned.1.call-done) | data formatting | bytes 8388608 | tf_op jit(solution)/shard_map/reshape | solution.py:73
  113.2 31.8 %all-gather.4.cloned.1.call-done = bf16[8192,256]{1,0:T(8,128)(2,1)} async-done(((bf16[512,256]{1,0:T(8,128)(2,1)}), bf16[8192,256]{1,0:T(8,128)(2,1)}) %all-gather.4.cloned.1.call-update) | async-done | bytes 4194320 | tf_op jit(solution)/shard_map/all_gather | solution.py:66
  145.0 6.9 %reshape.90 = bf16[16,512,2,128]{3,2,1,0:T(2,128)(2,1)} reshape(bf16[8192,256]{1,0:T(8,128)(2,1)} %all-gather.4.cloned.1.call-done) | data formatting | bytes 8388608 | tf_op jit(solution)/shard_map/reshape | solution.py:72
  151.9 184.2 %while.15 = (s32[]{:T(128)}, f32[2,4,512]{2,1,0:T(4,128)S(1)}, f32[2,4,512]{2,1,0:T(4,128)S(1)}, f32[2,4,512,128]{3,2,1,0:T(8,128)}, f32[16,512]{1,0:T(8,128)S(1...) while((s32[]{:T(128)}, f32[2,4,512]{2,1,0:T(4,128)S(1)}, ...), condition=%wide.region_9.10_spmd.clone, body=%wide.region_6.9_spmd.clone.sunk | while | flops 1103385600 | bytes 50086116 | solution.py:104
  154.8 1.6 fusion.44
  156.5 2.0 fusion.45
  158.5 3.5 %fusion.47 = f32[2,4,512,128]{3,2,1,0:T(8,128)S(1)} fusion(f32[2,4,512,128]{3,2,1,0:T(8,128)S(1)} %copy-done.1, f32[2,512,512,4]{2,1,3,0:T(8,128)S(1)} %get-tuple-element.250, f32[2,4,512]{2,1,0:T(4,128)S(1)} %select_maximum_fusion.2, pred[512,512]{0,1:T(8,128)(4,1)S(1)} %compare_and_fusion.2, f32[2,4,512]{2,1,0:T(4,128)S(1)} %get-tuple-element.252, ...), kind=kOutput, calls=%fused_computation.12.clone.1 | convolution fusion | flops 548929536 | bytes 13139969 | tf_op jit(solution)/shard_map/while/body/eval_jaxpr/qlwc,cqh->qlwh/dot_general | solution.py:95
  166.4 1.6 fusion.44
  168.0 2.0 fusion.45
  170.1 3.5 %fusion.47 = f32[2,4,512,128]{3,2,1,0:T(8,128)S(1)} fusion(f32[2,4,512,128]{3,2,1,0:T(8,128)S(1)} %copy-done.1, f32[2,512,512,4]{2,1,3,0:T(8,128)S(1)} %get-tuple-element.250, f32[2,4,512]{2,1,0:T(4,128)S(1)} %select_maximum_fusion.2, pred[512,512]{0,1:T(8,128)(4,1)S(1)} %compare_and_fusion.2, f32[2,4,512]{2,1,0:T(4,128)S(1)} %get-tuple-element.252, ...), kind=kOutput, calls=%fused_computation.12.clone.1 | convolution fusion | flops 548929536 | bytes 13139969 | tf_op jit(solution)/shard_map/while/body/eval_jaxpr/qlwc,cqh->qlwh/dot_general | solution.py:95
  177.9 1.6 fusion.44
  179.5 2.0 fusion.45
  181.6 3.5 %fusion.47 = f32[2,4,512,128]{3,2,1,0:T(8,128)S(1)} fusion(f32[2,4,512,128]{3,2,1,0:T(8,128)S(1)} %copy-done.1, f32[2,512,512,4]{2,1,3,0:T(8,128)S(1)} %get-tuple-element.250, f32[2,4,512]{2,1,0:T(4,128)S(1)} %select_maximum_fusion.2, pred[512,512]{0,1:T(8,128)(4,1)S(1)} %compare_and_fusion.2, f32[2,4,512]{2,1,0:T(4,128)S(1)} %get-tuple-element.252, ...), kind=kOutput, calls=%fused_computation.12.clone.1 | convolution fusion | flops 548929536 | bytes 13139969 | tf_op jit(solution)/shard_map/while/body/eval_jaxpr/qlwc,cqh->qlwh/dot_general | solution.py:95
  191.0 2.0 fusion.45
  193.1 3.5 %fusion.47 = f32[2,4,512,128]{3,2,1,0:T(8,128)S(1)} fusion(f32[2,4,512,128]{3,2,1,0:T(8,128)S(1)} %copy-done.1, f32[2,512,512,4]{2,1,3,0:T(8,128)S(1)} %get-tuple-element.250, f32[2,4,512]{2,1,0:T(4,128)S(1)} %select_maximum_fusion.2, pred[512,512]{0,1:T(8,128)(4,1)S(1)} %compare_and_fusion.2, f32[2,4,512]{2,1,0:T(4,128)S(1)} %get-tuple-element.252, ...), kind=kOutput, calls=%fused_computation.12.clone.1 | convolution fusion | flops 548929536 | bytes 13139969 | tf_op jit(solution)/shard_map/while/body/eval_jaxpr/qlwc,cqh->qlwh/dot_general | solution.py:95
  200.9 1.6 fusion.44
  202.5 2.0 fusion.45
  204.6 3.5 %fusion.47 = f32[2,4,512,128]{3,2,1,0:T(8,128)S(1)} fusion(f32[2,4,512,128]{3,2,1,0:T(8,128)S(1)} %copy-done.1, f32[2,512,512,4]{2,1,3,0:T(8,128)S(1)} %get-tuple-element.250, f32[2,4,512]{2,1,0:T(4,128)S(1)} %select_maximum_fusion.2, pred[512,512]{0,1:T(8,128)(4,1)S(1)} %compare_and_fusion.2, f32[2,4,512]{2,1,0:T(4,128)S(1)} %get-tuple-element.252, ...), kind=kOutput, calls=%fused_computation.12.clone.1 | convolution fusion | flops 548929536 | bytes 13139969 | tf_op jit(solution)/shard_map/while/body/eval_jaxpr/qlwc,cqh->qlwh/dot_general | solution.py:95
  212.4 1.6 fusion.44
  214.0 2.0 fusion.45
  216.1 3.5 %fusion.47 = f32[2,4,512,128]{3,2,1,0:T(8,128)S(1)} fusion(f32[2,4,512,128]{3,2,1,0:T(8,128)S(1)} %copy-done.1, f32[2,512,512,4]{2,1,3,0:T(8,128)S(1)} %get-tuple-element.250, f32[2,4,512]{2,1,0:T(4,128)S(1)} %select_maximum_fusion.2, pred[512,512]{0,1:T(8,128)(4,1)S(1)} %compare_and_fusion.2, f32[2,4,512]{2,1,0:T(4,128)S(1)} %get-tuple-element.252, ...), kind=kOutput, calls=%fused_computation.12.clone.1 | convolution fusion | flops 548929536 | bytes 13139969 | tf_op jit(solution)/shard_map/while/body/eval_jaxpr/qlwc,cqh->qlwh/dot_general | solution.py:95
  223.9 1.6 fusion.44
  225.6 2.0 fusion.45
  227.6 3.5 %fusion.47 = f32[2,4,512,128]{3,2,1,0:T(8,128)S(1)} fusion(f32[2,4,512,128]{3,2,1,0:T(8,128)S(1)} %copy-done.1, f32[2,512,512,4]{2,1,3,0:T(8,128)S(1)} %get-tuple-element.250, f32[2,4,512]{2,1,0:T(4,128)S(1)} %select_maximum_fusion.2, pred[512,512]{0,1:T(8,128)(4,1)S(1)} %compare_and_fusion.2, f32[2,4,512]{2,1,0:T(4,128)S(1)} %get-tuple-element.252, ...), kind=kOutput, calls=%fused_computation.12.clone.1 | convolution fusion | flops 548929536 | bytes 13139969 | tf_op jit(solution)/shard_map/while/body/eval_jaxpr/qlwc,cqh->qlwh/dot_general | solution.py:95
  235.5 1.6 fusion.44
  237.1 2.0 fusion.45
  239.2 3.5 %fusion.47 = f32[2,4,512,128]{3,2,1,0:T(8,128)S(1)} fusion(f32[2,4,512,128]{3,2,1,0:T(8,128)S(1)} %copy-done.1, f32[2,512,512,4]{2,1,3,0:T(8,128)S(1)} %get-tuple-element.250, f32[2,4,512]{2,1,0:T(4,128)S(1)} %select_maximum_fusion.2, pred[512,512]{0,1:T(8,128)(4,1)S(1)} %compare_and_fusion.2, f32[2,4,512]{2,1,0:T(4,128)S(1)} %get-tuple-element.252, ...), kind=kOutput, calls=%fused_computation.12.clone.1 | convolution fusion | flops 548929536 | bytes 13139969 | tf_op jit(solution)/shard_map/while/body/eval_jaxpr/qlwc,cqh->qlwh/dot_general | solution.py:95
  247.0 1.6 fusion.44
  248.6 2.0 fusion.45
  250.7 3.5 %fusion.47 = f32[2,4,512,128]{3,2,1,0:T(8,128)S(1)} fusion(f32[2,4,512,128]{3,2,1,0:T(8,128)S(1)} %copy-done.1, f32[2,512,512,4]{2,1,3,0:T(8,128)S(1)} %get-tuple-element.250, f32[2,4,512]{2,1,0:T(4,128)S(1)} %select_maximum_fusion.2, pred[512,512]{0,1:T(8,128)(4,1)S(1)} %compare_and_fusion.2, f32[2,4,512]{2,1,0:T(4,128)S(1)} %get-tuple-element.252, ...), kind=kOutput, calls=%fused_computation.12.clone.1 | convolution fusion | flops 548929536 | bytes 13139969 | tf_op jit(solution)/shard_map/while/body/eval_jaxpr/qlwc,cqh->qlwh/dot_general | solution.py:95
  258.5 1.6 fusion.44
  260.1 2.0 fusion.45
  262.2 3.5 %fusion.47 = f32[2,4,512,128]{3,2,1,0:T(8,128)S(1)} fusion(f32[2,4,512,128]{3,2,1,0:T(8,128)S(1)} %copy-done.1, f32[2,512,512,4]{2,1,3,0:T(8,128)S(1)} %get-tuple-element.250, f32[2,4,512]{2,1,0:T(4,128)S(1)} %select_maximum_fusion.2, pred[512,512]{0,1:T(8,128)(4,1)S(1)} %compare_and_fusion.2, f32[2,4,512]{2,1,0:T(4,128)S(1)} %get-tuple-element.252, ...), kind=kOutput, calls=%fused_computation.12.clone.1 | convolution fusion | flops 548929536 | bytes 13139969 | tf_op jit(solution)/shard_map/while/body/eval_jaxpr/qlwc,cqh->qlwh/dot_general | solution.py:95
  270.0 1.6 fusion.44
  271.6 2.0 fusion.45
  273.7 3.5 %fusion.47 = f32[2,4,512,128]{3,2,1,0:T(8,128)S(1)} fusion(f32[2,4,512,128]{3,2,1,0:T(8,128)S(1)} %copy-done.1, f32[2,512,512,4]{2,1,3,0:T(8,128)S(1)} %get-tuple-element.250, f32[2,4,512]{2,1,0:T(4,128)S(1)} %select_maximum_fusion.2, pred[512,512]{0,1:T(8,128)(4,1)S(1)} %compare_and_fusion.2, f32[2,4,512]{2,1,0:T(4,128)S(1)} %get-tuple-element.252, ...), kind=kOutput, calls=%fused_computation.12.clone.1 | convolution fusion | flops 548929536 | bytes 13139969 | tf_op jit(solution)/shard_map/while/body/eval_jaxpr/qlwc,cqh->qlwh/dot_general | solution.py:95
  281.5 1.6 fusion.44
  283.1 2.0 fusion.45
  285.2 3.5 %fusion.47 = f32[2,4,512,128]{3,2,1,0:T(8,128)S(1)} fusion(f32[2,4,512,128]{3,2,1,0:T(8,128)S(1)} %copy-done.1, f32[2,512,512,4]{2,1,3,0:T(8,128)S(1)} %get-tuple-element.250, f32[2,4,512]{2,1,0:T(4,128)S(1)} %select_maximum_fusion.2, pred[512,512]{0,1:T(8,128)(4,1)S(1)} %compare_and_fusion.2, f32[2,4,512]{2,1,0:T(4,128)S(1)} %get-tuple-element.252, ...), kind=kOutput, calls=%fused_computation.12.clone.1 | convolution fusion | flops 548929536 | bytes 13139969 | tf_op jit(solution)/shard_map/while/body/eval_jaxpr/qlwc,cqh->qlwh/dot_general | solution.py:95
  293.0 1.6 fusion.44
  294.7 2.0 fusion.45
  296.7 3.5 %fusion.47 = f32[2,4,512,128]{3,2,1,0:T(8,128)S(1)} fusion(f32[2,4,512,128]{3,2,1,0:T(8,128)S(1)} %copy-done.1, f32[2,512,512,4]{2,1,3,0:T(8,128)S(1)} %get-tuple-element.250, f32[2,4,512]{2,1,0:T(4,128)S(1)} %select_maximum_fusion.2, pred[512,512]{0,1:T(8,128)(4,1)S(1)} %compare_and_fusion.2, f32[2,4,512]{2,1,0:T(4,128)S(1)} %get-tuple-element.252, ...), kind=kOutput, calls=%fused_computation.12.clone.1 | convolution fusion | flops 548929536 | bytes 13139969 | tf_op jit(solution)/shard_map/while/body/eval_jaxpr/qlwc,cqh->qlwh/dot_general | solution.py:95
  304.6 1.6 fusion.44
  306.2 2.0 fusion.45
  308.3 3.5 %fusion.47 = f32[2,4,512,128]{3,2,1,0:T(8,128)S(1)} fusion(f32[2,4,512,128]{3,2,1,0:T(8,128)S(1)} %copy-done.1, f32[2,512,512,4]{2,1,3,0:T(8,128)S(1)} %get-tuple-element.250, f32[2,4,512]{2,1,0:T(4,128)S(1)} %select_maximum_fusion.2, pred[512,512]{0,1:T(8,128)(4,1)S(1)} %compare_and_fusion.2, f32[2,4,512]{2,1,0:T(4,128)S(1)} %get-tuple-element.252, ...), kind=kOutput, calls=%fused_computation.12.clone.1 | convolution fusion | flops 548929536 | bytes 13139969 | tf_op jit(solution)/shard_map/while/body/eval_jaxpr/qlwc,cqh->qlwh/dot_general | solution.py:95
  316.1 1.6 fusion.44
  317.7 2.0 fusion.45
  319.8 3.5 %fusion.47 = f32[2,4,512,128]{3,2,1,0:T(8,128)S(1)} fusion(f32[2,4,512,128]{3,2,1,0:T(8,128)S(1)} %copy-done.1, f32[2,512,512,4]{2,1,3,0:T(8,128)S(1)} %get-tuple-element.250, f32[2,4,512]{2,1,0:T(4,128)S(1)} %select_maximum_fusion.2, pred[512,512]{0,1:T(8,128)(4,1)S(1)} %compare_and_fusion.2, f32[2,4,512]{2,1,0:T(4,128)S(1)} %get-tuple-element.252, ...), kind=kOutput, calls=%fused_computation.12.clone.1 | convolution fusion | flops 548929536 | bytes 13139969 | tf_op jit(solution)/shard_map/while/body/eval_jaxpr/qlwc,cqh->qlwh/dot_general | solution.py:95
  327.6 1.6 fusion.44
  329.2 2.0 fusion.45
  331.3 3.5 %fusion.47 = f32[2,4,512,128]{3,2,1,0:T(8,128)S(1)} fusion(f32[2,4,512,128]{3,2,1,0:T(8,128)S(1)} %copy-done.1, f32[2,512,512,4]{2,1,3,0:T(8,128)S(1)} %get-tuple-element.250, f32[2,4,512]{2,1,0:T(4,128)S(1)} %select_maximum_fusion.2, pred[512,512]{0,1:T(8,128)(4,1)S(1)} %compare_and_fusion.2, f32[2,4,512]{2,1,0:T(4,128)S(1)} %get-tuple-element.252, ...), kind=kOutput, calls=%fused_computation.12.clone.1 | convolution fusion | flops 548929536 | bytes 13139969 | tf_op jit(solution)/shard_map/while/body/eval_jaxpr/qlwc,cqh->qlwh/dot_general | solution.py:95
  336.2 1.9 fusion.18
  (225 shorter events, 79.2 us)
Async XLA Ops:
  6.5 82.5 %copy-start = (bf16[1024,1024]{1,0:T(8,128)(2,1)S(1)}, bf16[1024,1024]{1,0:T(8,128)(2,1)}, u32[]{:S(2)}) copy-start(bf16[1024,1024]{1,0:T(8,128)(2,1)} %param.11) | copy-start | bytes 6291460
  12.0 12.3 %all-to-all-start = ((s32[16,1,64]{2,1,0:T(1,128)}), s32[16,1,64]{2,1,0:T(1,128)S(1)}, u32[]{:S(2)}, u32[]{:S(2)}) async-start(s32[16,1,64]{2,1,0:T(1,128)} %all_to_all.9), calls=%async_computation | async-start | bytes 16384 | tf_op jit(solution)/shard_map/all_to_all | solution.py:45
  24.4 43.6 %copy-start.3 = (s32[512]{0:T(512)S(1)}, s32[512]{0:T(512)}, u32[]{:S(2)}) copy-start(s32[512]{0:T(512)} %param.10) | copy-start | bytes 6148
  24.4 32.9 %all-to-all-start.1 = ((bf16[16,64,1024]{2,1,0:T(8,128)(2,1)}), bf16[16,64,1024]{2,1,0:T(8,128)(2,1)}, u32[]{:S(2)}, u32[]{:S(2)}) async-start(bf16[16,64,1024]{2,1,0:T(8,128)(2,1)} %bitcast.83), calls=%async_computation.1 | async-start | bytes 4194304 | tf_op jit(solution)/shard_map/all_to_all | solution.py:44
  29.6 76.7 %all-gather.6.cloned.1.call-start = ((), (), s32[]{:S(2)}) async-start(), calls=%async_computation.3 | async-start | bytes 4456448 | tf_op jit(solution)/shard_map/all_gather | solution.py:67
  65.7 79.3 %all-gather.4.cloned.1.call-start = ((), (), s32[]{:S(2)}) async-start(), calls=%async_computation.2 | async-start | bytes 4456448 | tf_op jit(solution)/shard_map/all_gather | solution.py:66
  156.4 2.1 copy-start.1
  162.1 1.4 copy-start.2
  168.0 2.1 copy-start.1
  173.6 1.4 copy-start.2
  179.5 2.1 copy-start.1
  185.1 1.4 copy-start.2
  191.0 2.1 copy-start.1
  196.6 1.4 copy-start.2
  202.5 2.1 copy-start.1
  208.1 1.4 copy-start.2
  214.0 2.1 copy-start.1
  219.6 1.4 copy-start.2
  225.5 2.1 copy-start.1
  231.2 1.4 copy-start.2
  237.1 2.1 copy-start.1
  242.7 1.4 copy-start.2
  248.6 2.1 copy-start.1
  254.2 1.4 copy-start.2
  260.1 2.1 copy-start.1
  265.7 1.4 copy-start.2
  271.6 2.1 copy-start.1
  277.2 1.4 copy-start.2
  283.1 2.1 copy-start.1
  288.7 1.4 copy-start.2
  294.6 2.1 copy-start.1
  300.3 1.4 copy-start.2
  306.1 2.1 copy-start.1
  311.8 1.4 copy-start.2
  317.7 2.1 copy-start.1
  323.3 1.4 copy-start.2
  329.2 2.1 copy-start.1
  334.8 1.4 copy-start.2
Sparse Core Ops, SparseCore 0:
  65.8 40.4 all-gather.5
  108.0 36.9 all-gather.3
where the time goes:
time: 349 us; the launch traced here: 347 us
  local copies, waits for them, and re-layouts  88.4 us (25%)
  matrix products  88.2 us (25%)
  waiting for transfers between devices  70 us (20%)
  other arithmetic  52.9 us (15%)
  blocking collectives  21 us (6%)
  between operations  13.5 us (4%)
  starting transfers between devices  12.2 us (3%)
    dot_general x16, matrix products, one_block(): jnp.einsum('qlwc,cqh->qlwh', softmax_weights.astype(jnp.bfloat16), value_...  56.2 us
    reduce_sum x16, other arithmetic, one_block(): total_tokens = total_tokens * shrink + jnp.sum(softmax_weights, axis=-1)  32.7 us
    all_gather x1, waiting for transfers between devices, on_device(): key_portion = lax.all_gather(key_rows, 'ctx', axis=0, tiled=True)  31.8 us
    dynamic_slice x48, local copies, waits for them, and re-layouts, on_device(): lax.scan(one_block, carry, (key_block_list, value_block_list, seg_blocks,...  31.8 us
    all_to_all x1, waiting for transfers between devices, on_device(): lax.all_to_all(send_rows, 'ctx', split_axis=0, concat_axis=0, tiled=True)  26.4 us
    dot_general x16, matrix products, one_block(): jnp.einsum('qxli,oxi->xlqo', query_head_rows, key_tile_rows, preferred_el...  25.3 us
    while x80, local copies, waits for them, and re-layouts  21.6 us
    all_gather x1, blocking collectives, on_device(): seg_piece = lax.all_gather(seg_sent, 'ctx', axis=0, tiled=True)  21 us
  transfers between devices with their start and end apart: 4, of which 4 were waited for; matrix products, arithmetic and copies ran while one was open for 6% of the time, Pallas kernels for 0%

commit v1 on v0

--- a/solution.py
+++ b/solution.py
@@ -63,7 +63,9 @@
         jnp.zeros((KEY_VALUE_HEADS, group_size, token_count, HEAD_SIZE), jnp.float32),
     )
     carry = start_state
-    key_portion = lax.all_gather(key_rows, "ctx", axis=0, tiled=True)
+    key_portion = jnp.concatenate(
+        lax.all_to_all(jnp.stack([key_rows] * lax.axis_size("ctx")), "ctx", 0, 0), axis=0
+    )
     value_portion = lax.all_gather(value_rows, "ctx", axis=0, tiled=True)
     seg_piece = lax.all_gather(seg_sent, "ctx", axis=0, tiled=True)
     token_rows = key_portion.shape[0]

time: 349 us -> 385 us (1.10)
  blocking collectives: 21 us -> 85.2 us
  waiting for transfers between devices: 70 us -> 27.1 us
  matrix products: 88.2 us -> 104 us
  local copies, waits for them, and re-layouts: 88.4 us -> 79.7 us
  starting transfers between devices: 12.2 us -> 18.4 us
    all_gather x1, blocking collectives: 21 us -> 85.2 us  [on_device(): seg_piece = lax.all_gather(seg_sent, 'ctx', axis=0, tiled=True)]
    all_gather x1 -> x0, waiting for transfers between devices: 31.8 us -> none  [on_device(): key_portion = lax.all_gather(key_rows, 'ctx', axis=0, tiled=True)]
    dot_general x16, matrix products: 25.3 us -> 41.7 us  [one_block(): jnp.einsum('qxli,oxi->xlqo', query_head_rows, key_tile_rows, preferred_el...]
    all_gather x1, waiting for transfers between devices: 11.1 us -> 0.02 us  [on_device(): value_portion = lax.all_gather(value_rows, 'ctx', axis=0, tiled=True)]
    reshape x1 -> x0, local copies, waits for them, and re-layouts: 6.92 us -> none  [on_device(): key_portion.reshape(event_count, block_step, KEY_VALUE_HEADS, HEAD_SIZE)]
    all_to_all x0 -> x1, starting transfers between devices: none -> 6.39 us  [on_device(): lax.all_to_all(jnp.stack([key_rows] * lax.axis_size('ctx')), 'ctx', 0, 0)]
    dynamic_slice x48, local copies, waits for them, and re-layouts: 31.8 us -> 27.6 us  [on_device(): lax.scan(one_block, carry, (key_block_list, value_block_list, seg_blocks,...]
  transfers between devices with their start and end apart: 4 -> 4, of which waited for: 4 -> 2; matrix products, arithmetic and copies ran while one was open for 6% -> 6% of each run, Pallas kernels for 0% -> 0%
where the time goes in v1:
time: 385 us; the launch traced here: 382 us
  matrix products  104 us (27%)
  blocking collectives  85.2 us (22%)
  local copies, waits for them, and re-layouts  79.7 us (21%)
  other arithmetic  52.9 us (14%)
  waiting for transfers between devices  27.1 us (7%)
  starting transfers between devices  18.4 us (5%)
  between operations  13.6 us (4%)
    all_gather x1, blocking collectives, on_device(): seg_piece = lax.all_gather(seg_sent, 'ctx', axis=0, tiled=True)  85.2 us
    dot_general x16, matrix products, one_block(): jnp.einsum('qlwc,cqh->qlwh', softmax_weights.astype(jnp.bfloat16), value_...  56.2 us
    dot_general x16, matrix products, one_block(): jnp.einsum('qxli,oxi->xlqo', query_head_rows, key_tile_rows, preferred_el...  41.7 us
    reduce_sum x16, other arithmetic, one_block(): total_tokens = total_tokens * shrink + jnp.sum(softmax_weights, axis=-1)  32.7 us
    dynamic_slice x48, local copies, waits for them, and re-layouts, on_device(): lax.scan(one_block, carry, (key_block_list, value_block_list, seg_blocks,...  27.6 us
    all_to_all x1, waiting for transfers between devices, on_device(): lax.all_to_all(send_rows, 'ctx', split_axis=0, concat_axis=0, tiled=True)  26.4 us
    while x80, local copies, waits for them, and re-layouts  21.4 us
    add x16, other arithmetic, on_device(): own_position = myself * token_count + local_rows  10.3 us
  transfers between devices with their start and end apart: 4, of which 2 were waited for; matrix products, arithmetic and copies ran while one was open for 6% of the time, Pallas kernels for 0%

profile of v1, /device:TPU:1, one launch (start us, length us, event | category | flops | bytes accessed | tf_op | source)
XLA Modules:
  0.0 382.2 jit_solution(14803848642137771946)
XLA Ops:
  8.9 2.4 scatter_custom_fusion
  12.0 6.9 %all-to-all-start = ((s32[16,1,64]{2,1,0:T(1,128)}), s32[16,1,64]{2,1,0:T(1,128)S(1)}, u32[]{:S(2)}, u32[]{:S(2)}) async-start(s32[16,1,64]{2,1,0:T(1,128)} %all_to_all.12), calls=%async_computation | async-start | bytes 16384 | tf_op jit(solution)/shard_map/all_to_all | solution.py:45
  18.9 4.8 %scatter_custom_fusion.1 = bf16[1024,1024]{1,0:T(8,128)(2,1)} fusion(s32[512]{0:T(512)S(1)} %compare_select_fusion.1, bf16[512,1024]{1,0:T(8,128)(2,1)} %param.8, bf16[]{:T(256)} %constant.62.clone.1), kind=kCustom, calls=%fused_computation.34 | custom fusion | bytes 2097664 | tf_op jit(solution)/shard_map/scatter | solution.py:34
  24.4 5.1 %all-to-all-start.1 = ((bf16[16,64,1024]{2,1,0:T(8,128)(2,1)}), bf16[16,64,1024]{2,1,0:T(8,128)(2,1)}, u32[]{:S(2)}, u32[]{:S(2)}) async-start(bf16[16,64,1024]{2,1,0:T(8,128)(2,1)} %bitcast.85), calls=%async_computation.1 | async-start | bytes 4194304 | tf_op jit(solution)/shard_map/all_to_all | solution.py:44
  30.8 26.4 %all-to-all-done.1 = bf16[16,64,1024]{2,1,0:T(8,128)(2,1)} async-done(((bf16[16,64,1024]{2,1,0:T(8,128)(2,1)}), bf16[16,64,1024]{2,1,0:T(8,128)(2,1)}, u32[]{:S(2)}, u32[]{:S(2)}) %all-to-all-start.1) | async-done | bytes 2097184 | tf_op jit(solution)/shard_map/all_to_all | solution.py:44
  57.1 6.2 %scatter_custom_fusion.2 = bf16[512,1024]{1,0:T(8,128)(2,1)S(1)} fusion(s32[1024]{0:T(1024)S(1)} %bitcast.89, bf16[1024,1024]{1,0:T(8,128)(2,1)} %bitcast.4, bf16[]{:T(256)} %constant.62.clone.1), kind=kCustom, calls=%fused_computation.37 | custom fusion | bytes 1049088 | tf_op jit(solution)/shard_map/scatter | solution.py:50
  63.3 2.6 convolution_convert_fusion.1
  67.5 2.4 stack.2
  69.9 6.4 %all-to-all-start.2 = ((bf16[16,512,256]{1,2,0:T(8,128)(2,1)}), bf16[16,512,256]{1,2,0:T(8,128)(2,1)}, u32[]{:S(2)}, u32[]{:S(2)}) async-start(bf16[16,512,256]{1,2,0:T(8,128)(2,1)} %stack.2), calls=%async_computation.2 | async-start | bytes 8388608 | tf_op jit(solution)/shard_map/all_to_all | solution.py:67
  76.4 85.2 %all-gather = bf16[16,1,512]{2,1,0:T(2,128)(2,1)S(1)} all-gather(bf16[1,1,512]{2,1,0:T(2,128)(2,1)S(1)} %reshape.119), channel_id=1, replica_groups=mesh['dp'=8,'ctx'=16] {'ctx'}, dimensions={0}, use_global_device_ids=true | all-gather | bytes 17408 | tf_op jit(solution)/shard_map/all_gather | solution.py:70
  161.6 2.2 convolution_convert_fusion
  163.9 2.6 reshape.89
  167.8 6.9 %reshape.90 = bf16[16,512,2,128]{3,2,1,0:T(2,128)(2,1)} reshape(bf16[8192,256]{1,0:T(8,128)(2,1)} %all-gather.3.cloned.1.call-done) | data formatting | bytes 8388608 | tf_op jit(solution)/shard_map/reshape | solution.py:75
  174.8 196.3 %while.15 = (s32[]{:T(128)}, f32[2,4,512]{2,1,0:T(4,128)S(1)}, f32[2,4,512]{2,1,0:T(4,128)S(1)}, f32[2,4,512,128]{3,2,1,0:T(8,128)}, f32[16,512]{1,0:T(8,128)S(1...) while((s32[]{:T(128)}, f32[2,4,512]{2,1,0:T(4,128)S(1)}, ...), condition=%wide.region_9.10_spmd.clone, body=%wide.region_6.9_spmd.clone.sunk | while | flops 1103385600 | bytes 49561832 | solution.py:106
  177.4 2.6 fusion.47
  180.1 2.0 fusion.48
  182.2 3.5 fusion.50
  189.7 2.6 fusion.47
  192.3 2.0 fusion.48
  194.4 3.5 fusion.50
  202.0 2.6 fusion.47
  204.6 2.0 fusion.48
  206.7 3.5 fusion.50
  214.2 2.6 fusion.47
  216.9 2.0 fusion.48
  219.0 3.5 fusion.50
  226.5 2.6 fusion.47
  229.2 2.0 fusion.48
  231.2 3.5 fusion.50
  238.8 2.6 fusion.47
  241.4 2.0 fusion.48
  243.5 3.5 fusion.50
  251.1 2.6 fusion.47
  253.7 2.0 fusion.48
  255.8 3.5 fusion.50
  263.3 2.6 fusion.47
  266.0 2.0 fusion.48
  268.1 3.5 fusion.50
  275.6 2.6 fusion.47
  278.2 2.0 fusion.48
  280.3 3.5 fusion.50
  287.9 2.6 fusion.47
  290.5 2.0 fusion.48
  292.6 3.5 fusion.50
  300.1 2.6 fusion.47
  302.8 2.0 fusion.48
  304.9 3.5 fusion.50
  312.4 2.6 fusion.47
  315.0 2.0 fusion.48
  317.1 3.5 fusion.50
  324.7 2.6 fusion.47
  327.3 2.0 fusion.48
  329.4 3.5 fusion.50
  336.9 2.6 fusion.47
  339.6 2.0 fusion.48
  341.7 3.5 fusion.50
  349.2 2.6 fusion.47
  351.9 2.0 fusion.48
  353.9 3.5 fusion.50
  361.5 2.6 fusion.47
  364.1 2.0 fusion.48
  366.2 3.5 fusion.50
  371.1 1.9 fusion.21
  373.9 1.5 convert_element_type.44
  (229 shorter events, 73.3 us)
Async XLA Ops:
  6.5 155.1 %copy-start = (bf16[1024,1024]{1,0:T(8,128)(2,1)S(1)}, bf16[1024,1024]{1,0:T(8,128)(2,1)}, u32[]{:S(2)}) copy-start(bf16[1024,1024]{1,0:T(8,128)(2,1)} %param.11) | copy-start | bytes 6291460
  12.0 12.3 %all-to-all-start = ((s32[16,1,64]{2,1,0:T(1,128)}), s32[16,1,64]{2,1,0:T(1,128)S(1)}, u32[]{:S(2)}, u32[]{:S(2)}) async-start(s32[16,1,64]{2,1,0:T(1,128)} %all_to_all.12), calls=%async_computation | async-start | bytes 16384 | tf_op jit(solution)/shard_map/all_to_all | solution.py:45
  24.4 32.8 %all-to-all-start.1 = ((bf16[16,64,1024]{2,1,0:T(8,128)(2,1)}), bf16[16,64,1024]{2,1,0:T(8,128)(2,1)}, u32[]{:S(2)}, u32[]{:S(2)}) async-start(bf16[16,64,1024]{2,1,0:T(8,128)(2,1)} %bitcast.85), calls=%async_computation.1 | async-start | bytes 4194304 | tf_op jit(solution)/shard_map/all_to_all | solution.py:44
  29.4 138.4 %all-gather.3.cloned.1.call-start = ((), (), s32[]{:S(2)}) async-start(), calls=%async_computation.3 | async-start | bytes 4456448 | tf_op jit(solution)/shard_map/all_gather | solution.py:69
  63.3 2.6 copy-start.3
  69.9 6.4 %copy-start.5 = (s32[512]{0:T(512)S(1)}, s32[512]{0:T(512)}, u32[]{:S(2)}) copy-start(s32[512]{0:T(512)} %param.10) | copy-start | bytes 6148
  69.9 91.7 %copy-start.4 = (bf16[512,1024]{1,0:T(8,128)(2,1)S(1)}, bf16[512,1024]{1,0:T(8,128)(2,1)}, u32[]{:S(2)}) copy-start(bf16[512,1024]{1,0:T(8,128)(2,1)} %copy-done.3) | copy-start | bytes 3145732
  69.9 104.9 %all-to-all-start.2 = ((bf16[16,512,256]{1,2,0:T(8,128)(2,1)}), bf16[16,512,256]{1,2,0:T(8,128)(2,1)}, u32[]{:S(2)}, u32[]{:S(2)}) async-start(bf16[16,512,256]{1,2,0:T(8,128)(2,1)} %stack.2), calls=%async_computation.2 | async-start | bytes 8388608 | tf_op jit(solution)/shard_map/all_to_all | solution.py:67
  180.1 2.1 copy-start.1
  185.7 1.4 copy-start.2
  192.3 2.1 copy-start.1
  198.0 1.4 copy-start.2
  204.6 2.1 copy-start.1
  210.2 1.4 copy-start.2
  216.9 2.1 copy-start.1
  222.5 1.4 copy-start.2
  229.1 2.1 copy-start.1
  234.8 1.4 copy-start.2
  241.4 2.1 copy-start.1
  247.0 1.4 copy-start.2
  253.7 2.1 copy-start.1
  259.3 1.4 copy-start.2
  266.0 2.1 copy-start.1
  271.6 1.4 copy-start.2
  278.2 2.1 copy-start.1
  283.8 1.4 copy-start.2
  290.5 2.1 copy-start.1
  296.1 1.4 copy-start.2
  302.8 2.1 copy-start.1
  308.4 1.4 copy-start.2
  315.0 2.1 copy-start.1
  320.7 1.4 copy-start.2
  327.3 2.1 copy-start.1
  332.9 1.4 copy-start.2
  339.6 2.1 copy-start.1
  345.2 1.4 copy-start.2
  351.8 2.1 copy-start.1
  357.5 1.4 copy-start.2
  364.1 2.1 copy-start.1
  369.7 1.4 copy-start.2
Sparse Core Ops, SparseCore 0:
  66.0 84.0 all-gather.2
